TPU v7x, 32 devices: a whole 2x2x4 slice. The times are simulated.
32 devices in a mesh: gx: 4 (over z), gy: 8 (over y, x, core).
Axes of the slice: x: 2, y: 2, z: 4, core: 2. Of those that a mesh axis runs over, the one named last changes fastest.
Arguments:
- coeffs: bfloat16 [8, 64, 256, 128], P('gx', 'gy'), may hold values from -0.25 to 0.25
- permit: float32 [8, 64, 256], P('gx', 'gy'), may hold values from 0.25 to 4
- shift_diag: float32 [8, 64, 128], P('gx', 'gy'), may hold values from 0.5 to 4
- codes: int32 [8, 64, 6], P('gx', 'gy'), may hold values from 0 to 8
- counts: int32 [8, 64], P('gx', 'gy'), may hold values from 1 to 6
- weights: float32 [8, 64, 6], P('gx', 'gy'), may hold values from 0.5 to 1.5
- vectors: bfloat16 [8, 64, 128, 128], P('gx', 'gy'), may hold values from -6 to 6
Outputs:
- factor: bfloat16 [8, 64, 128, 128], P('gx', 'gy')
- applied: bfloat16 [8, 64, 128, 128], P('gx', 'gy')
All inputs are finite; a program needn't handle non-finite values.
Results may differ from a plain program's by a relative error of at most 0.0051.
Values may be sent and summed in bfloat16 or wider, within the bound.
A program may use at most 64 MiB of HBM per device.

v0:
```python
import functools

import jax
import jax.numpy as jnp
from jax import lax
from jax.experimental import pallas as pl
from jax.experimental.pallas import tpu as pltpu
from jax.sharding import PartitionSpec as P

MESH = pl.DeviceIdType.MESH
BASE = 32
DIRS = ((1, 0), (-1, 0), (0, 1), (0, -1), (1, 1), (1, -1), (-1, 1), (-1, -1))


def neighbours():
    sizes = (lax.axis_size("gx"), lax.axis_size("gy"))
    me = (lax.axis_index("gx"), lax.axis_index("gy"))

    def there(d):
        return (me[0] + d[0], me[1] + d[1])

    def exists(d):
        ok = None
        for size, at, step in zip(sizes, me, d):
            if step == 0:
                continue
            test = (at + 1 < size) if step > 0 else (at > 0)
            ok = test if ok is None else jnp.logical_and(ok, test)
        return ok

    return there, exists


def gram_kernel(c_ref, permit_ref, shift_ref, codes_ref, counts_ref, weights_ref, gram_ref, wt, cs, ts, own_sem, send_sem, recv_sem):
    bx, by, coupling, order = c_ref.shape
    slots = codes_ref.shape[0]
    wide = by + 2
    there, exists = neighbours()
    row = {1: bx - 1, -1: 0}
    col = {1: by - 1, -1: 0}
    land_row = {1: 0, -1: bx + 1}
    land_col = {1: 0, -1: by + 1}
    gx_dirs, gy_dirs, corners = DIRS[:2], DIRS[2:4], DIRS[4:]
    own = [pltpu.make_async_copy(c_ref.at[x], cs.at[pl.ds((x + 1) * wide + 1, by)], own_sem.at[x]) for x in range(bx)]
    for copy in own:
        copy.start()
    barrier = pltpu.get_barrier_semaphore()
    for d in DIRS:
        @pl.when(exists(d))
        def _(d=d):
            pl.semaphore_signal(barrier, inc=1, device_id=there(d), device_id_type=MESH)
    near = [exists(d).astype(jnp.int32) for d in DIRS[:4]]
    pl.semaphore_wait(barrier, (near[0] + near[1] + 1) * (near[2] + near[3] + 1) - 1)

    def remote(source, target, k, d):
        return pltpu.make_async_remote_copy(
            src_ref=source, dst_ref=cs.at[target], send_sem=send_sem.at[k], recv_sem=recv_sem.at[k],
            device_id=there(d), device_id_type=MESH)

    def gy_copy(j, x):
        d = gy_dirs[j]
        return remote(c_ref.at[x, col[d[1]]], (x + 1) * wide + land_col[d[1]], 4 + j * bx + x, d)

    def corner_copy(j):
        d = corners[j]
        return remote(c_ref.at[row[d[0]], col[d[1]]], land_row[d[0]] * wide + land_col[d[1]], j, d)

    def gx_copy(j, y):
        d = gx_dirs[j]
        return remote(c_ref.at[row[d[0]], y], land_row[d[0]] * wide + y + 1, 4 + 2 * bx + 2 * y + j, d)

    for j, d in enumerate(corners):
        @pl.when(exists(d))
        def _(j=j):
            corner_copy(j).start()
    for j, d in enumerate(gx_dirs):
        @pl.when(exists(d))
        def _(j=j):
            for y in range(by):
                gx_copy(j, y).start()
    for j, d in enumerate(gy_dirs):
        @pl.when(exists(d))
        def _(j=j):
            for x in range(bx):
                gy_copy(j, x).start()

    zero = jnp.zeros((coupling, order), cs.dtype)
    for j, d in enumerate(corners):
        @pl.when(jnp.logical_not(exists((-d[0], -d[1]))))
        def _(d=d):
            cs[land_row[d[0]] * wide + land_col[d[1]]] = zero
    for j, d in enumerate(gx_dirs):
        @pl.when(jnp.logical_not(exists((-d[0], -d[1]))))
        def _(d=d):
            @pl.loop(0, by)
            def _(y):
                cs[land_row[d[0]] * wide + y + 1] = zero
    for j, d in enumerate(gy_dirs):
        @pl.when(jnp.logical_not(exists((-d[0], -d[1]))))
        def _(d=d):
            for x in range(bx):
                cs[(x + 1) * wide + land_col[d[1]]] = zero

    def turn(n):
        ts[n] = cs[n].T

    def terms(x, y, pairs):
        p = permit_ref[x, pl.ds(y, 1), :]
        acc = None
        for ax, ay in pairs:
            n = (x + ax) * wide + y + ay
            times = jnp.int32(0)
            for s in range(slots):
                hit = (codes_ref[s, x, y] == ax * 3 + ay) & (s < counts_ref[x, y])
                times = times + hit.astype(jnp.int32)
            scaled = (ts[n].astype(jnp.float32) * p).astype(jnp.bfloat16)
            term = times.astype(jnp.float32) * jnp.dot(scaled, cs[n], preferred_element_type=jnp.float32)
            acc = term if acc is None else acc + term
        return acc

    inside = {x: [ax for ax in range(3) if 0 <= x + ax - 1 < bx] for x in range(bx)}
    outside = {x: [ax for ax in range(3) if not 0 <= x + ax - 1 < bx] for x in range(bx)}

    @pl.loop(0, by)
    def _(y):
        for x in range(bx):
            for offset in range(9):
                w = jnp.float32(0.0)
                for s in range(slots):
                    hit = (codes_ref[s, x, y] == offset) & (s < counts_ref[x, y])
                    w = w + jnp.where(hit, weights_ref[s, x, y], 0.0)
                wt[offset, x * by + y] = w

    for copy in own:
        copy.wait()
    for x in range(bx):
        @pl.loop(0, by)
        def _(y):
            turn((x + 1) * wide + y + 1)
    for x in range(bx):
        @pl.loop(1, by - 1)
        def _(y):
            gram_ref[x, y] = terms(x, y, [(ax, ay) for ax in inside[x] for ay in range(3)])
    for j, d in enumerate(gy_dirs):
        @pl.when(exists((-d[0], -d[1])))
        def _(j=j):
            for x in range(bx):
                gy_copy(j, x).wait_recv()
    for x in range(bx):
        turn((x + 1) * wide)
        turn((x + 1) * wide + by + 1)
    for x in range(bx):
        @pl.loop(0, 2)
        def _(e):
            y = e * (by - 1)
            gram_ref[x, y] = terms(x, y, [(ax, ay) for ax in inside[x] for ay in range(3)])

    same = lax.broadcasted_iota(jnp.int32, (order, order), 0) == lax.broadcasted_iota(jnp.int32, (order, order), 1)

    def finished(x, y, acc):
        gram_ref[x, y] = 0.5 * (acc + acc.T) + jnp.where(same, shift_ref[x, pl.ds(y, 1), :], 0.0)

    for x in range(1, bx - 1):
        @pl.loop(0, by)
        def _(y):
            finished(x, y, gram_ref[x, y])
    for j, d in enumerate(corners):
        @pl.when(exists((-d[0], -d[1])))
        def _(j=j):
            corner_copy(j).wait_recv()
    for r in (0, bx + 1):
        turn(r * wide)
        turn(r * wide + by + 1)

    def arrive(y):
        for j, d in enumerate(gx_dirs):
            @pl.when(exists((-d[0], -d[1])))
            def _(j=j):
                gx_copy(j, y).wait_recv()
        turn(y + 1)
        turn((bx + 1) * wide + y + 1)

    def last(y):
        for x in sorted({0, bx - 1}):
            finished(x, y, gram_ref[x, y] + terms(x, y, [(ax, ay) for ax in outside[x] for ay in range(3)]))

    arrive(0)

    @pl.loop(1, by)
    def _(y):
        arrive(y)
        last(y - 1)

    last(by - 1)
    for j, d in enumerate(corners):
        @pl.when(exists(d))
        def _(j=j):
            corner_copy(j).wait_send()
    for j, d in enumerate(gx_dirs):
        @pl.when(exists(d))
        def _(j=j):
            for y in range(by):
                gx_copy(j, y).wait_send()
    for j, d in enumerate(gy_dirs):
        @pl.when(exists(d))
        def _(j=j):
            for x in range(bx):
                gy_copy(j, x).wait_send()


def factor_kernel(gram_ref, fac_ref, gs):
    bx, by, order = gram_ref.shape[:3]
    blocks = bx * by
    for i in range(blocks):
        gs[i] = gram_ref[i // by, i % by]

    lanes = lax.broadcasted_iota(jnp.int32, (order, order), 1)
    per = order // BASE
    seg = lax.broadcasted_iota(jnp.int32, (BASE, order), 1) // BASE
    place = lax.broadcasted_iota(jnp.int32, (BASE, order), 1) % BASE
    row = lax.broadcasted_iota(jnp.int32, (BASE, order), 0)
    for stage in range(per):
        low = stage * BASE
        high = low + BASE
        packs = []
        for g in range(blocks // per):
            pack = None
            for q in range(per):
                piece = gs[g * per + q, low:high, :]
                shift = (q * BASE - low) % order
                piece = pltpu.roll(piece, shift, axis=1) if shift else piece
                pack = piece if pack is None else jnp.where(seg == q, piece, pack)
            packs.append(pack)
        done = [[] for _ in packs]
        scale = [[] for _ in packs]
        for k in range(0, BASE, 2):
            top = k // 8 * 8
            at, nxt = k - top, k + 1 - top
            for g, m in enumerate(packs):
                f = jnp.take_along_axis(m, seg[top:] * BASE + k, axis=1)
                f_next = jnp.take_along_axis(m, seg[top:] * BASE + (k + 1), axis=1)
                d = f[at:at + 1]
                inv_d = 1.0 / d
                scale[g].append(lax.rsqrt(d))
                f = jnp.where(row[top:] > k, f, 0.0)
                f_next = f_next - f * (f_next[at:at + 1] * inv_d)
                d_next = f_next[nxt:nxt + 1]
                scale[g].append(lax.rsqrt(d_next))
                m = m - f * ((m[at:at + 1] + jnp.where(place[:1] == k, 1.0, 0.0)) * inv_d)
                f_next = jnp.where(row[top:] > k + 1, f_next, 0.0)
                r_next = m[nxt:nxt + 1] + jnp.where(place[:1] == k + 1, 1.0, 0.0)
                m = m - f_next * (r_next * (1.0 / d_next))
                if k % 8 == 6:
                    done[g].append(m[:8])
                    m = m[8:]
                packs[g] = m
        for g in range(len(packs)):
            m = jnp.concatenate(done[g], axis=0)
            unit = jnp.where(row > place, m, jnp.where(row == place, 1.0, 0.0))
            inv = unit * jnp.concatenate(scale[g], axis=0)
            wide_inv = jnp.concatenate([jnp.where(seg == q, inv, 0.0) for q in range(per)], axis=0)
            panel = []
            for q in range(per):
                here = gs[g * per + q, low:high, :]
                panel.append(jnp.where(seg == stage, jnp.where(row == place, 1.0, 0.0), here))
            panel = jnp.concatenate(panel, axis=0)
            whole = jnp.dot(wide_inv, panel, precision=lax.Precision.HIGHEST, preferred_element_type=jnp.float32)
            for q in range(per):
                at = g * per + q
                part = whole[q * BASE:(q + 1) * BASE]
                gs[at, low:high, :] = jnp.where(seg <= stage, part, 0.0)
                if high < order:
                    h = part.astype(jnp.bfloat16)
                    rest = part - h.astype(jnp.float32)
                    m = rest.astype(jnp.bfloat16)
                    l = (rest - m.astype(jnp.float32)).astype(jnp.bfloat16)
                    update = lax.dot_general(
                        jnp.concatenate([h, h, m, h, l, m], axis=0), jnp.concatenate([h, m, h, l, h, m], axis=0),
                        (((0,), (0,)), ((), ())), preferred_element_type=jnp.float32)
                    below = gs[at, high:, :]
                    below = jnp.where(lanes[high:] // BASE == stage, 0.0, below)
                    gs[at, high:, :] = below - update[high:]

    @pl.loop(0, blocks)
    def _(i):
        fac_ref[i // by, i % by] = gs[i].astype(fac_ref.dtype)


def sum_kernel(fac_ref, v_ref, wt, out_ref, img, loc, px, py, pc, rx, ry, rc, send_sem, recv_sem):
    bx, by = fac_ref.shape[:2]
    there, exists = neighbours()
    sends = [px.at[0], px.at[1], py.at[0], py.at[1]] + [pc.at[k] for k in range(4)]
    lands = [rx.at[0], rx.at[1], ry.at[0], ry.at[1]] + [rc.at[k] for k in range(4)]
    barrier = pltpu.get_barrier_semaphore()
    for d in DIRS:
        @pl.when(exists(d))
        def _(d=d):
            pl.semaphore_signal(barrier, inc=1, device_id=there(d), device_id_type=MESH)
    for k, d in enumerate(DIRS):
        @pl.when(jnp.logical_not(exists((-d[0], -d[1]))))
        def _(k=k):
            lands[k][...] = jnp.zeros(lands[k].shape, lands[k].dtype)

    @pl.loop(0, by)
    def _(y):
        for x in range(bx):
            img[x, y] = lax.dot_general(fac_ref[x, y], v_ref[x, y], (((0,), (0,)), ((), ())),
                                        preferred_element_type=jnp.float32)

    def target(tx, ty):
        total = None
        for x in range(bx):
            for y in range(by):
                ax, ay = tx - x, ty - y
                if 0 <= ax < 3 and 0 <= ay < 3:
                    term = wt[ax * 3 + ay, x * by + y] * img[x, y]
                    total = term if total is None else total + term
        return total

    for y in range(by):
        px[0, y] = target(bx + 1, y + 1).astype(px.dtype)
        px[1, y] = target(0, y + 1).astype(px.dtype)
    for k, d in enumerate(DIRS[4:]):
        pc[k] = target(bx + 1 if d[0] > 0 else 0, by + 1 if d[1] > 0 else 0).astype(pc.dtype)
    for x in range(bx):
        py[0, x] = target(x + 1, by + 1).astype(py.dtype)
        py[1, x] = target(x + 1, 0).astype(py.dtype)
    near = [exists(d).astype(jnp.int32) for d in DIRS[:4]]
    pl.semaphore_wait(barrier, (near[0] + near[1] + 1) * (near[2] + near[3] + 1) - 1)

    def copy(k, d):
        return pltpu.make_async_remote_copy(
            src_ref=sends[k], dst_ref=lands[k], send_sem=send_sem.at[k], recv_sem=recv_sem.at[k],
            device_id=there(d), device_id_type=MESH)

    order_of = (4, 5, 6, 7, 0, 1, 2, 3)
    for k in order_of:
        @pl.when(exists(DIRS[k]))
        def _(k=k):
            copy(k, DIRS[k]).start()
    for x in range(bx):
        for y in range(by):
            loc[x, y] = target(x + 1, y + 1)
    for k in order_of:
        @pl.when(exists((-DIRS[k][0], -DIRS[k][1])))
        def _(k=k):
            copy(k, DIRS[k]).wait_recv()
    for x in range(bx):
        for y in range(by):
            total = loc[x, y]
            for k, edge in ((0, 0), (1, bx - 1)):
                if x == edge:
                    total = total + rx[k, y].astype(jnp.float32)
            for k, edge in ((0, 0), (1, by - 1)):
                if y == edge:
                    total = total + ry[k, x].astype(jnp.float32)
            for k, place in enumerate(((0, 0), (0, by - 1), (bx - 1, 0), (bx - 1, by - 1))):
                if (x, y) == place:
                    total = total + rc[k].astype(jnp.float32)
            out_ref[x, y] = total.astype(out_ref.dtype)
    for k in order_of:
        @pl.when(exists(DIRS[k]))
        def _(k=k):
            copy(k, DIRS[k]).wait_send()


def local(coeffs, permit, shift_diag, codes, counts, weights, vectors):
    bx, by, coupling, order = coeffs.shape
    nv = vectors.shape[3]
    bf16, f32 = jnp.bfloat16, jnp.float32
    anyspace = pl.BlockSpec(memory_space=pl.ANY)
    vmem = pl.BlockSpec(memory_space=pltpu.VMEM)
    smem = pl.BlockSpec(memory_space=pltpu.SMEM)
    codes, weights = jnp.transpose(codes, (2, 0, 1)), jnp.transpose(weights, (2, 0, 1))
    padded = (bx + 2) * (by + 2)
    copies = 4 + 2 * bx + 2 * by
    gram, sums = pl.pallas_call(
        gram_kernel,
        out_shape=(jax.ShapeDtypeStruct((bx, by, order, order), f32), jax.ShapeDtypeStruct((9, bx * by), f32)),
        in_specs=[anyspace, vmem, vmem, smem, smem, smem],
        out_specs=(vmem, smem),
        scratch_shapes=[
            pltpu.VMEM((padded, coupling, order), bf16),
            pltpu.VMEM((padded, order, coupling), bf16),
            pltpu.SemaphoreType.DMA((bx,)),
            pltpu.SemaphoreType.DMA((copies,)), pltpu.SemaphoreType.DMA((copies,)),
        ],
        compiler_params=pltpu.CompilerParams(collective_id=0, has_side_effects=True),
        name="gram",
    )(coeffs, permit, shift_diag, codes, counts, weights)
    fac = pl.pallas_call(
        factor_kernel,
        out_shape=jax.ShapeDtypeStruct((bx, by, order, order), bf16),
        in_specs=[vmem],
        out_specs=vmem,
        scratch_shapes=[pltpu.VMEM((bx * by, order, order), f32)],
        name="factor",
    )(gram)
    edges = [
        pltpu.VMEM((2, by, order, nv), bf16),
        pltpu.VMEM((2, bx, order, nv), bf16),
        pltpu.VMEM((4, order, nv), bf16),
    ]
    applied = pl.pallas_call(
        sum_kernel,
        out_shape=jax.ShapeDtypeStruct((bx, by, order, nv), bf16),
        in_specs=[vmem, vmem, smem],
        out_specs=vmem,
        scratch_shapes=[
            pltpu.VMEM((bx, by, order, nv), f32),
            pltpu.VMEM((bx, by, order, nv), f32),
            *edges, *edges,
            pltpu.SemaphoreType.DMA((8,)), pltpu.SemaphoreType.DMA((8,)),
        ],
        compiler_params=pltpu.CompilerParams(collective_id=1, has_side_effects=True),
        name="sums",
    )(fac, vectors, sums)
    return fac, applied


def solution(mesh):
    placed = (
        P("gx", "gy", None, None),
        P("gx", "gy", None),
        P("gx", "gy", None),
        P("gx", "gy", None),
        P("gx", "gy"),
        P("gx", "gy", None),
        P("gx", "gy", None, None),
    )
    return jax.shard_map(
        local,
        mesh=mesh,
        in_specs=placed,
        out_specs=(P("gx", "gy", None, None), P("gx", "gy", None, None)),
        check_vma=False,
    )
```

profile of v0, /device:TPU:4, one launch (start us, length us, event | category | flops | bytes accessed | tf_op | source)
XLA Modules:
  0.0 53.5 jit_solution(15650402568262015923)
XLA Ops:
  0.6 22.4 %gram.1 = (f32[2,8,128,128]{3,2,1,0:T(8,128)}, f32[9,16]{1,0:T(8,128)}) custom-call(bf16[2,8,256,128]{3,2,1,0:T(8,128)(2,1)} %c_ref.1, f32[2,8,256]{2,1,0:T(8,128)} %permit_ref.1, f32[2,8,128]{2,1,0:T(8,128)} %shift_ref.1, s32[6,2,8]{2,1,0:T(2,128)} %bitcast.2, s32[2,8]{1,0:T(2,128)} %counts_ref.1, f32[6,2,8]{2,1,0:T(2,128)} %bitcast.3), custom_call_target="tpu_custom_call" | custom-call | tf_op jit(solution)/shard_map/gram/pallas_call | solution.py:377
  23.1 14.8 %factor.1.fac_ref = bf16[2,8,128,128]{3,2,1,0:T(8,128)(2,1)} custom-call(f32[2,8,128,128]{3,2,1,0:T(8,128)} %get-tuple-element.4.gram_ref), custom_call_target="tpu_custom_call" | custom-call | tf_op jit(solution)/shard_map/factor/pallas_call | solution.py:391
  37.9 13.7 %sums.1 = bf16[2,8,128,128]{3,2,1,0:T(8,128)(2,1)} custom-call(bf16[2,8,128,128]{3,2,1,0:T(8,128)(2,1)} %factor.1.fac_ref, bf16[2,8,128,128]{3,2,1,0:T(8,128)(2,1)} %v_ref.1, f32[9,16]{1,0:T(8,128)} %get-tuple-element.5.wt), custom_call_target="tpu_custom_call" | custom-call | tf_op jit(solution)/shard_map/sums/pallas_call | solution.py:404
  51.6 1.9 %copy.10 = bf16[2,8,128,128]{3,2,1,0:T(8,128)(2,1)} copy(bf16[2,8,128,128]{3,2,1,0:T(8,128)(2,1)} %sums.1) | data formatting | bytes 1048576
where the time goes:
time: 53.8 us; the launch traced here: 53.5 us
  Pallas kernels  50.9 us (95%)
  local copies, waits for them, and re-layouts  1.89 us (4%)
  between operations  0.65 us (1%)
    pallas_call x1, Pallas kernels, local(): pl.pallas_call(gram_kernel, out_shape=(jax.ShapeDtypeStruct((bx, by, orde...  22.4 us
    pallas_call x1, Pallas kernels, local(): pl.pallas_call(factor_kernel, out_shape=jax.ShapeDtypeStruct((bx, by, ord...  14.8 us
    pallas_call x1, Pallas kernels, local(): pl.pallas_call(sum_kernel, out_shape=jax.ShapeDtypeStruct((bx, by, order,...  13.7 us
    unnamed x1, local copies, waits for them, and re-layouts  1.89 us

commit v1 on v0

--- a/solution.py
+++ b/solution.py
@@ -9,6 +9,7 @@
 
 MESH = pl.DeviceIdType.MESH
 BASE = 32
+WIDTH = 4
 DIRS = ((1, 0), (-1, 0), (0, 1), (0, -1), (1, 1), (1, -1), (-1, 1), (-1, -1))
 
 
@@ -208,82 +209,91 @@
                 gy_copy(j, x).wait_send()
 
 
-def factor_kernel(gram_ref, fac_ref, gs):
+def split(x):
+    h = x.astype(jnp.bfloat16)
+    return h, (x - h.astype(jnp.float32)).astype(jnp.bfloat16)
+
+
+def factor_kernel(gram_ref, out_ref, fac_ref, gs, sem):
     bx, by, order = gram_ref.shape[:3]
     blocks = bx * by
     for i in range(blocks):
         gs[i] = gram_ref[i // by, i % by]
-
+    factor(gs, fac_ref, bx, by, order)
+    copy = pltpu.make_async_copy(fac_ref, out_ref, sem)
+    copy.start()
+    copy.wait()
+
+
+def factor(gs, fac_ref, bx, by, order):
+    blocks = bx * by
     lanes = lax.broadcasted_iota(jnp.int32, (order, order), 1)
     per = order // BASE
     seg = lax.broadcasted_iota(jnp.int32, (BASE, order), 1) // BASE
     place = lax.broadcasted_iota(jnp.int32, (BASE, order), 1) % BASE
     row = lax.broadcasted_iota(jnp.int32, (BASE, order), 0)
+    seg8, place8, row8 = seg[:8], place[:8], row[:8]
+    masks = [jnp.where(seg == q, 1.0, 0.0).astype(jnp.bfloat16) for q in range(per)]
+    tops = BASE // 8
+    groups = blocks // per
     for stage in range(per):
         low = stage * BASE
         high = low + BASE
         packs = []
-        for g in range(blocks // per):
+        for g in range(groups):
             pack = None
             for q in range(per):
                 piece = gs[g * per + q, low:high, :]
                 shift = (q * BASE - low) % order
                 piece = pltpu.roll(piece, shift, axis=1) if shift else piece
                 pack = piece if pack is None else jnp.where(seg == q, piece, pack)
-            packs.append(pack)
-        done = [[] for _ in packs]
-        scale = [[] for _ in packs]
-        for k in range(0, BASE, 2):
-            top = k // 8 * 8
-            at, nxt = k - top, k + 1 - top
-            for g, m in enumerate(packs):
-                f = jnp.take_along_axis(m, seg[top:] * BASE + k, axis=1)
-                f_next = jnp.take_along_axis(m, seg[top:] * BASE + (k + 1), axis=1)
-                d = f[at:at + 1]
-                inv_d = 1.0 / d
-                scale[g].append(lax.rsqrt(d))
-                f = jnp.where(row[top:] > k, f, 0.0)
-                f_next = f_next - f * (f_next[at:at + 1] * inv_d)
-                d_next = f_next[nxt:nxt + 1]
-                scale[g].append(lax.rsqrt(d_next))
-                m = m - f * ((m[at:at + 1] + jnp.where(place[:1] == k, 1.0, 0.0)) * inv_d)
-                f_next = jnp.where(row[top:] > k + 1, f_next, 0.0)
-                r_next = m[nxt:nxt + 1] + jnp.where(place[:1] == k + 1, 1.0, 0.0)
-                m = m - f_next * (r_next * (1.0 / d_next))
-                if k % 8 == 6:
-                    done[g].append(m[:8])
-                    m = m[8:]
-                packs[g] = m
-        for g in range(len(packs)):
-            m = jnp.concatenate(done[g], axis=0)
+            packs.append([pack[8 * c:8 * c + 8] for c in range(tops)])
+        pivots = [[jnp.ones((8, order), jnp.float32) for _ in range(tops)] for _ in range(groups)]
+        for first in range(0, BASE, WIDTH):
+            top = first // 8
+            cols = [[[jnp.take_along_axis(m[c], seg8 * BASE + (first + j), axis=1) for c in range(top, tops)]
+                     for j in range(WIDTH)] for m in packs]
+            for j in range(WIDTH):
+                k = first + j
+                at = k - 8 * top
+                for g, m in enumerate(packs):
+                    f = cols[g][j]
+                    d = jnp.broadcast_to(f[0][at:at + 1], (8, order))
+                    inv_d = 1.0 / d
+                    pivots[g][top] = jnp.where(row8 == at, d, pivots[g][top])
+                    f = [jnp.where(row8 > at, f[0], 0.0)] + f[1:]
+                    for n in range(j + 1, WIDTH):
+                        t = jnp.broadcast_to(cols[g][n][0][at:at + 1], (8, order)) * inv_d
+                        cols[g][n] = [x - y * t for x, y in zip(cols[g][n], f)]
+                    r = (jnp.broadcast_to(m[top][at:at + 1], (8, order)) + jnp.where(place8 == k, 1.0, 0.0)) * inv_d
+                    for c in range(top, tops):
+                        m[c] = m[c] - f[c - top] * r
+        for g, m in enumerate(packs):
+            m = jnp.concatenate(m, axis=0)
             unit = jnp.where(row > place, m, jnp.where(row == place, 1.0, 0.0))
-            inv = unit * jnp.concatenate(scale[g], axis=0)
-            wide_inv = jnp.concatenate([jnp.where(seg == q, inv, 0.0) for q in range(per)], axis=0)
+            inv = unit * lax.rsqrt(jnp.concatenate(pivots[g], axis=0))
+            inv_h, inv_l = split(inv)
+            wide_h = jnp.concatenate([inv_h * mask for mask in masks], axis=0)
+            wide_l = jnp.concatenate([inv_l * mask for mask in masks], axis=0)
             panel = []
             for q in range(per):
                 here = gs[g * per + q, low:high, :]
                 panel.append(jnp.where(seg == stage, jnp.where(row == place, 1.0, 0.0), here))
-            panel = jnp.concatenate(panel, axis=0)
-            whole = jnp.dot(wide_inv, panel, precision=lax.Precision.HIGHEST, preferred_element_type=jnp.float32)
+            panel_h, panel_l = split(jnp.concatenate(panel, axis=0))
+            whole = jnp.dot(jnp.concatenate([wide_h, wide_h, wide_l], axis=1),
+                            jnp.concatenate([panel_h, panel_l, panel_h], axis=0),
+                            preferred_element_type=jnp.float32)
             for q in range(per):
                 at = g * per + q
                 part = whole[q * BASE:(q + 1) * BASE]
-                gs[at, low:high, :] = jnp.where(seg <= stage, part, 0.0)
+                fac_ref[at // by, at % by, low:high, :] = jnp.where(seg <= stage, part, 0.0).astype(fac_ref.dtype)
                 if high < order:
-                    h = part.astype(jnp.bfloat16)
-                    rest = part - h.astype(jnp.float32)
-                    m = rest.astype(jnp.bfloat16)
-                    l = (rest - m.astype(jnp.float32)).astype(jnp.bfloat16)
-                    update = lax.dot_general(
-                        jnp.concatenate([h, h, m, h, l, m], axis=0), jnp.concatenate([h, m, h, l, h, m], axis=0),
-                        (((0,), (0,)), ((), ())), preferred_element_type=jnp.float32)
+                    h, l = split(part)
+                    left = jnp.concatenate([h, h, l], axis=0).T
+                    update = jnp.dot(left[high:], jnp.concatenate([h, l, h], axis=0), preferred_element_type=jnp.float32)
                     below = gs[at, high:, :]
                     below = jnp.where(lanes[high:] // BASE == stage, 0.0, below)
-                    gs[at, high:, :] = below - update[high:]
-
-    @pl.loop(0, blocks)
-    def _(i):
-        fac_ref[i // by, i % by] = gs[i].astype(fac_ref.dtype)
+                    gs[at, high:, :] = below - update
 
 
 def sum_kernel(fac_ref, v_ref, wt, out_ref, img, loc, px, py, pc, rx, ry, rc, send_sem, recv_sem):
@@ -376,7 +386,7 @@
     copies = 4 + 2 * bx + 2 * by
     gram, sums = pl.pallas_call(
         gram_kernel,
-        out_shape=(jax.ShapeDtypeStruct((bx, by, order, order), f32), jax.ShapeDtypeStruct((9, bx * by), f32)),
+        out_shape=(pltpu.VMEM((bx, by, order, order), f32), jax.ShapeDtypeStruct((9, bx * by), f32)),
         in_specs=[anyspace, vmem, vmem, smem, smem, smem],
         out_specs=(vmem, smem),
         scratch_shapes=[
@@ -388,14 +398,14 @@
         compiler_params=pltpu.CompilerParams(collective_id=0, has_side_effects=True),
         name="gram",
     )(coeffs, permit, shift_diag, codes, counts, weights)
-    fac = pl.pallas_call(
+    fac, held = pl.pallas_call(
         factor_kernel,
-        out_shape=jax.ShapeDtypeStruct((bx, by, order, order), bf16),
+        out_shape=(jax.ShapeDtypeStruct((bx, by, order, order), bf16), pltpu.VMEM((bx, by, order, order), bf16)),
         in_specs=[vmem],
-        out_specs=vmem,
-        scratch_shapes=[pltpu.VMEM((bx * by, order, order), f32)],
+        out_specs=(anyspace, vmem),
+        scratch_shapes=[pltpu.VMEM((bx * by, order, order), f32), pltpu.SemaphoreType.DMA],
         name="factor",
-    )(gram)
+    )(pltpu.with_memory_space_constraint(gram, pltpu.VMEM))
     edges = [
         pltpu.VMEM((2, by, order, nv), bf16),
         pltpu.VMEM((2, bx, order, nv), bf16),
@@ -403,7 +413,7 @@
     ]
     applied = pl.pallas_call(
         sum_kernel,
-        out_shape=jax.ShapeDtypeStruct((bx, by, order, nv), bf16),
+        out_shape=pltpu.VMEM((bx, by, order, nv), bf16),
         in_specs=[vmem, vmem, smem],
         out_specs=vmem,
         scratch_shapes=[
@@ -414,7 +424,7 @@
         ],
         compiler_params=pltpu.CompilerParams(collective_id=1, has_side_effects=True),
         name="sums",
-    )(fac, vectors, sums)
+    )(pltpu.with_memory_space_constraint(held, pltpu.VMEM), vectors, sums)
     return fac, applied
 
 

time: 53.8 us -> 45.6 us (0.85)
  Pallas kernels: 50.9 us -> 44 us
  local copies, waits for them, and re-layouts: 1.89 us -> 0.8 us
    pallas_call x3, Pallas kernels: 50.9 us -> 44 us  [the longest x1 22.1 us: local(): pl.pallas_call(gram_kernel, out_shape=(pltpu.VMEM((bx, by, order, order),...]
    unnamed x1, local copies, waits for them, and re-layouts: 1.89 us -> 0.8 us
where the time goes in v1:
time: 45.6 us; the launch traced here: 45.4 us
  Pallas kernels  44 us (96%)
  local copies, waits for them, and re-layouts  0.8 us (2%)
  between operations  0.66 us (1%)
    pallas_call x1, Pallas kernels, local(): pl.pallas_call(gram_kernel, out_shape=(pltpu.VMEM((bx, by, order, order),...  22.1 us
    pallas_call x1, Pallas kernels, local(): pl.pallas_call(sum_kernel, out_shape=pltpu.VMEM((bx, by, order, nv), bf16...  12.8 us
    pallas_call x1, Pallas kernels, local(): pl.pallas_call(factor_kernel, out_shape=(jax.ShapeDtypeStruct((bx, by, or...  9.14 us

profile of v1, /device:TPU:4, one launch (start us, length us, event | category | flops | bytes accessed | tf_op | source)
XLA Modules:
  0.0 45.4 jit_solution(7767065869137959796)
XLA Ops:
  0.6 22.1 %gram.1 = (f32[2,8,128,128]{3,2,1,0:T(8,128)S(1)}, f32[9,16]{1,0:T(8,128)}) custom-call(bf16[2,8,256,128]{3,2,1,0:T(8,128)(2,1)} %c_ref.1, f32[2,8,256]{2,1,0:T(8,128)} %permit_ref.1, f32[2,8,128]{2,1,0:T(8,128)} %shift_ref.1, s32[6,2,8]{2,1,0:T(2,128)} %bitcast.2, s32[2,8]{1,0:T(2,128)} %counts_ref.1, f32[6,2,8]{2,1,0:T(2,128)} %bitcast.3), custom_call_target="tpu_custom_call" | custom-call | tf_op jit(solution)/shard_map/gram/pallas_call | solution.py:387
  22.7 9.1 %factor.1 = (bf16[2,8,128,128]{3,2,1,0:T(8,128)(2,1)}, bf16[2,8,128,128]{3,2,1,0:T(8,128)(2,1)S(1)}) custom-call(f32[2,8,128,128]{3,2,1,0:T(8,128)S(1)} %get-tuple-element.6.gram_ref), custom_call_target="tpu_custom_call" | custom-call | tf_op jit(solution)/shard_map/factor/pallas_call | solution.py:401
  31.9 12.8 %sums.1 = bf16[2,8,128,128]{3,2,1,0:T(8,128)(2,1)S(1)} custom-call(bf16[2,8,128,128]{3,2,1,0:T(8,128)(2,1)S(1)} %get-tuple-element.8.fac_ref, bf16[2,8,128,128]{3,2,1,0:T(8,128)(2,1)} %v_ref.1, f32[9,16]{1,0:T(8,128)} %get-tuple-element.9.wt), custom_call_target="tpu_custom_call" | custom-call | tf_op jit(solution)/shard_map/sums/pallas_call | solution.py:414
  44.6 0.8 %copy.10 = bf16[2,8,128,128]{3,2,1,0:T(8,128)(2,1)} copy(bf16[2,8,128,128]{3,2,1,0:T(8,128)(2,1)S(1)} %sums.1) | data formatting | bytes 1048576

commit v2 on v1

--- a/solution.py
+++ b/solution.py
@@ -32,53 +32,74 @@
     return there, exists
 
 
-def gram_kernel(c_ref, permit_ref, shift_ref, codes_ref, counts_ref, weights_ref, gram_ref, wt, cs, ts, own_sem, send_sem, recv_sem):
+def gram_kernel(c_ref, permit_ref, shift_ref, codes_ref, counts_ref, weights_ref, gram_ref, wrow_ref,
+                cs, ts, pm, sh, cd, ct, wg, flat, tp, tq, ps, pr, own_sem, in_sem, send_sem, recv_sem):
     bx, by, coupling, order = c_ref.shape
     slots = codes_ref.shape[0]
     wide = by + 2
+    quarter = order // 4
+    packed = pr.shape[2]
     there, exists = neighbours()
-    row = {1: bx - 1, -1: 0}
-    col = {1: by - 1, -1: 0}
-    land_row = {1: 0, -1: bx + 1}
-    land_col = {1: 0, -1: by + 1}
-    gx_dirs, gy_dirs, corners = DIRS[:2], DIRS[2:4], DIRS[4:]
-    own = [pltpu.make_async_copy(c_ref.at[x], cs.at[pl.ds((x + 1) * wide + 1, by)], own_sem.at[x]) for x in range(bx)]
-    for copy in own:
-        copy.start()
+    edge = {1: by - 1, -1: 0}
+    land = {1: 0, -1: by + 1}
+    gx_dirs, gy_dirs = DIRS[:2], DIRS[2:4]
+    small = [pltpu.make_async_copy(source, target, in_sem.at[k]) for k, (source, target) in enumerate((
+        (codes_ref, cd), (counts_ref, ct), (weights_ref, wg), (permit_ref, pm), (shift_ref, sh)))]
+    own = [pltpu.make_async_copy(c_ref.at[x], cs.at[pl.ds(x * wide + 1, by)], own_sem.at[x]) for x in range(bx)]
     barrier = pltpu.get_barrier_semaphore()
-    for d in DIRS:
+    for d in DIRS[:4]:
         @pl.when(exists(d))
         def _(d=d):
             pl.semaphore_signal(barrier, inc=1, device_id=there(d), device_id_type=MESH)
-    near = [exists(d).astype(jnp.int32) for d in DIRS[:4]]
-    pl.semaphore_wait(barrier, (near[0] + near[1] + 1) * (near[2] + near[3] + 1) - 1)
+    for copy in small + own:
+        copy.start()
 
     def remote(source, target, k, d):
         return pltpu.make_async_remote_copy(
-            src_ref=source, dst_ref=cs.at[target], send_sem=send_sem.at[k], recv_sem=recv_sem.at[k],
+            src_ref=source, dst_ref=target, send_sem=send_sem.at[k], recv_sem=recv_sem.at[k],
             device_id=there(d), device_id_type=MESH)
 
     def gy_copy(j, x):
         d = gy_dirs[j]
-        return remote(c_ref.at[x, col[d[1]]], (x + 1) * wide + land_col[d[1]], 4 + j * bx + x, d)
-
-    def corner_copy(j):
-        d = corners[j]
-        return remote(c_ref.at[row[d[0]], col[d[1]]], land_row[d[0]] * wide + land_col[d[1]], j, d)
-
-    def gx_copy(j, y):
-        d = gx_dirs[j]
-        return remote(c_ref.at[row[d[0]], y], land_row[d[0]] * wide + y + 1, 4 + 2 * bx + 2 * y + j, d)
-
-    for j, d in enumerate(corners):
-        @pl.when(exists(d))
-        def _(j=j):
-            corner_copy(j).start()
+        return remote(c_ref.at[x, edge[d[1]]], cs.at[x * wide + land[d[1]]], j * bx + x, d)
+
+    def scale_copy(j):
+        x, o = ((bx - 1, 6), (0, 0))[j]
+        return remote(tp.at[x, pl.ds(o, 3)], tq.at[j], 2 * bx + j, gx_dirs[j])
+
+    def part_copy(j, y):
+        return remote(ps.at[j, y], pr.at[j, y], 2 * bx + 2 + j * by + y, gx_dirs[1 - j])
+
+    for copy in small[:4]:
+        copy.wait()
+    flat[...] = jnp.zeros(flat.shape, flat.dtype)
+    half = order // 2
+    for o in range(9):
+        times = jnp.zeros((bx, by), jnp.float32)
+        total = jnp.zeros((bx, by), jnp.float32)
+        for s in range(slots):
+            hit = (cd[s] == o) & (s < ct[...])
+            times = times + jnp.where(hit, 1.0, 0.0)
+            total = total + jnp.where(hit, wg[s], 0.0)
+        flat[o * bx:(o + 1) * bx, 0:by] = times
+        flat[half + o * bx:half + (o + 1) * bx, 0:by] = total
+    turned = flat[...].T[0:by]
+
+    def column(c):
+        return jnp.take_along_axis(turned, jnp.full((by, order), c, jnp.int32), axis=1)
+
+    for o in (6, 7, 8, 0, 1, 2, 3, 4, 5):
+        for x in range(bx):
+            times = column(o * bx + x)
+            tp[x, o] = pm[x] * jnp.concatenate([times] * (coupling // order), axis=1)
+            wrow_ref[o, x] = column(half + o * bx + x)
+
+    near = [exists(d).astype(jnp.int32) for d in DIRS[:4]]
+    pl.semaphore_wait(barrier, near[0] + near[1] + near[2] + near[3])
     for j, d in enumerate(gx_dirs):
         @pl.when(exists(d))
         def _(j=j):
-            for y in range(by):
-                gx_copy(j, y).start()
+            scale_copy(j).start()
     for j, d in enumerate(gy_dirs):
         @pl.when(exists(d))
         def _(j=j):
@@ -86,124 +107,115 @@
                 gy_copy(j, x).start()
 
     zero = jnp.zeros((coupling, order), cs.dtype)
-    for j, d in enumerate(corners):
-        @pl.when(jnp.logical_not(exists((-d[0], -d[1]))))
-        def _(d=d):
-            cs[land_row[d[0]] * wide + land_col[d[1]]] = zero
-    for j, d in enumerate(gx_dirs):
-        @pl.when(jnp.logical_not(exists((-d[0], -d[1]))))
-        def _(d=d):
-            @pl.loop(0, by)
-            def _(y):
-                cs[land_row[d[0]] * wide + y + 1] = zero
     for j, d in enumerate(gy_dirs):
         @pl.when(jnp.logical_not(exists((-d[0], -d[1]))))
         def _(d=d):
             for x in range(bx):
-                cs[(x + 1) * wide + land_col[d[1]]] = zero
+                cs[x * wide + land[d[1]]] = zero
 
     def turn(n):
         ts[n] = cs[n].T
 
-    def terms(x, y, pairs):
-        p = permit_ref[x, pl.ds(y, 1), :]
-        acc = None
-        for ax, ay in pairs:
-            n = (x + ax) * wide + y + ay
-            times = jnp.int32(0)
-            for s in range(slots):
-                hit = (codes_ref[s, x, y] == ax * 3 + ay) & (s < counts_ref[x, y])
-                times = times + hit.astype(jnp.int32)
-            scaled = (ts[n].astype(jnp.float32) * p).astype(jnp.bfloat16)
-            term = times.astype(jnp.float32) * jnp.dot(scaled, cs[n], preferred_element_type=jnp.float32)
-            acc = term if acc is None else acc + term
-        return acc
-
-    inside = {x: [ax for ax in range(3) if 0 <= x + ax - 1 < bx] for x in range(bx)}
-    outside = {x: [ax for ax in range(3) if not 0 <= x + ax - 1 < bx] for x in range(bx)}
-
-    @pl.loop(0, by)
-    def _(y):
+    def terms(r, y, scales):
+        left = jnp.concatenate([(ts[r * wide + y + ay].astype(jnp.float32) * scales(ay)).astype(jnp.bfloat16)
+                                for ay in range(3)], axis=1)
+        right = cs[pl.ds(r * wide + y, 3)].reshape(3 * coupling, order)
+        return jnp.dot(left, right, preferred_element_type=jnp.float32)
+
+    same = lax.broadcasted_iota(jnp.int32, (order, order), 0) == lax.broadcasted_iota(jnp.int32, (order, order), 1)
+
+    def inner(y):
         for x in range(bx):
-            for offset in range(9):
-                w = jnp.float32(0.0)
-                for s in range(slots):
-                    hit = (codes_ref[s, x, y] == offset) & (s < counts_ref[x, y])
-                    w = w + jnp.where(hit, weights_ref[s, x, y], 0.0)
-                wt[offset, x * by + y] = w
+            acc = jnp.where(same, sh[x, pl.ds(y, 1), :], 0.0)
+            for r in range(max(0, x - 1), min(bx, x + 2)):
+                acc = acc + terms(r, y, lambda ay: tp[x, (r - x + 1) * 3 + ay, pl.ds(y, 1), :])
+            gram_ref[x, y] = acc
+
+    lane = lax.broadcasted_iota(jnp.int32, (quarter, order), 1)
+
+    def outer(j, y):
+        acc = terms((0, bx - 1)[j], y, lambda ay: tq[j, ay, pl.ds(y, 1), :])
+        ps[j, y, 0:quarter] = acc[0:quarter]
+        ps[j, y, quarter:2 * quarter] = jnp.where(
+            lane < quarter, pltpu.roll(acc[3 * quarter:], quarter, axis=1), acc[quarter:2 * quarter])
+        mid = 2 * quarter + quarter // 2
+        ps[j, y, 2 * quarter:mid] = jnp.where(
+            lane[:quarter // 2] < 2 * quarter, pltpu.roll(acc[mid:3 * quarter], 2 * quarter, axis=1), acc[2 * quarter:mid])
+
+    def send(j, y):
+        @pl.when(exists(gx_dirs[1 - j]))
+        def _():
+            part_copy(j, y).start()
 
     for copy in own:
         copy.wait()
+    small[4].wait()
     for x in range(bx):
-        @pl.loop(0, by)
+        @pl.loop(0, by, unroll=2)
         def _(y):
-            turn((x + 1) * wide + y + 1)
-    for x in range(bx):
-        @pl.loop(1, by - 1)
-        def _(y):
-            gram_ref[x, y] = terms(x, y, [(ax, ay) for ax in inside[x] for ay in range(3)])
+            turn(x * wide + y + 1)
+    split_at = by // 2
+
+    @pl.loop(1, split_at)
+    def _(y):
+        inner(y)
+
+    for j in range(2):
+        @pl.when(exists(gx_dirs[1 - j]))
+        def _(j=j):
+            scale_copy(j).wait_recv()
+    for y in range(1, by - 1):
+        for j in range(2):
+            outer(j, y)
+        for j in range(2):
+            send(j, y)
     for j, d in enumerate(gy_dirs):
         @pl.when(exists((-d[0], -d[1])))
         def _(j=j):
             for x in range(bx):
                 gy_copy(j, x).wait_recv()
     for x in range(bx):
-        turn((x + 1) * wide)
-        turn((x + 1) * wide + by + 1)
-    for x in range(bx):
-        @pl.loop(0, 2)
-        def _(e):
-            y = e * (by - 1)
-            gram_ref[x, y] = terms(x, y, [(ax, ay) for ax in inside[x] for ay in range(3)])
-
-    same = lax.broadcasted_iota(jnp.int32, (order, order), 0) == lax.broadcasted_iota(jnp.int32, (order, order), 1)
-
-    def finished(x, y, acc):
-        gram_ref[x, y] = 0.5 * (acc + acc.T) + jnp.where(same, shift_ref[x, pl.ds(y, 1), :], 0.0)
-
-    for x in range(1, bx - 1):
-        @pl.loop(0, by)
-        def _(y):
-            finished(x, y, gram_ref[x, y])
-    for j, d in enumerate(corners):
-        @pl.when(exists((-d[0], -d[1])))
-        def _(j=j):
-            corner_copy(j).wait_recv()
-    for r in (0, bx + 1):
-        turn(r * wide)
-        turn(r * wide + by + 1)
-
-    def arrive(y):
-        for j, d in enumerate(gx_dirs):
-            @pl.when(exists((-d[0], -d[1])))
-            def _(j=j):
-                gx_copy(j, y).wait_recv()
-        turn(y + 1)
-        turn((bx + 1) * wide + y + 1)
-
-    def last(y):
-        for x in sorted({0, bx - 1}):
-            finished(x, y, gram_ref[x, y] + terms(x, y, [(ax, ay) for ax in outside[x] for ay in range(3)]))
-
-    arrive(0)
-
-    @pl.loop(1, by)
+        turn(x * wide)
+        turn(x * wide + by + 1)
+    for y in sorted({0, by - 1}):
+        for j in range(2):
+            outer(j, y)
+        for j in range(2):
+            send(j, y)
+
+    @pl.loop(split_at, by - 1)
     def _(y):
-        arrive(y)
-        last(y - 1)
-
-    last(by - 1)
-    for j, d in enumerate(corners):
-        @pl.when(exists(d))
-        def _(j=j):
-            corner_copy(j).wait_send()
-    for j, d in enumerate(gx_dirs):
-        @pl.when(exists(d))
+        inner(y)
+
+    @pl.loop(0, 2)
+    def _(e):
+        inner(e * (by - 1))
+
+    mid = 2 * quarter + quarter // 2
+    for y in list(range(1, by - 1)) + sorted({0, by - 1}):
+        for j in range(2):
+            @pl.when(exists(gx_dirs[j]))
+            def _(j=j, y=y):
+                part_copy(j, y).wait_recv()
+                x = (bx - 1, 0)[j]
+                gram_ref[x, y, 0:quarter] += pr[j, y, 0:quarter]
+                both = pr[j, y, quarter:2 * quarter]
+                gram_ref[x, y, quarter:2 * quarter] += both
+                gram_ref[x, y, 3 * quarter:] += pltpu.roll(both, 3 * quarter, axis=1)
+                both = pr[j, y, 2 * quarter:mid]
+                gram_ref[x, y, 2 * quarter:mid] += both
+                gram_ref[x, y, mid:3 * quarter] += pltpu.roll(both, 2 * quarter, axis=1)
+    for j in range(2):
+        @pl.when(exists(gx_dirs[j]))
+        def _(j=j):
+            scale_copy(j).wait_send()
+
+        @pl.when(exists(gx_dirs[1 - j]))
         def _(j=j):
             for y in range(by):
-                gx_copy(j, y).wait_send()
-    for j, d in enumerate(gy_dirs):
-        @pl.when(exists(d))
+                part_copy(j, y).wait_send()
+
+        @pl.when(exists(gy_dirs[j]))
         def _(j=j):
             for x in range(bx):
                 gy_copy(j, x).wait_send()
@@ -323,7 +335,7 @@
             for y in range(by):
                 ax, ay = tx - x, ty - y
                 if 0 <= ax < 3 and 0 <= ay < 3:
-                    term = wt[ax * 3 + ay, x * by + y] * img[x, y]
+                    term = wt[ax * 3 + ay, x, pl.ds(y, 1), :] * img[x, y]
                     total = term if total is None else total + term
         return total
 
@@ -380,19 +392,24 @@
     bf16, f32 = jnp.bfloat16, jnp.float32
     anyspace = pl.BlockSpec(memory_space=pl.ANY)
     vmem = pl.BlockSpec(memory_space=pltpu.VMEM)
-    smem = pl.BlockSpec(memory_space=pltpu.SMEM)
     codes, weights = jnp.transpose(codes, (2, 0, 1)), jnp.transpose(weights, (2, 0, 1))
-    padded = (bx + 2) * (by + 2)
-    copies = 4 + 2 * bx + 2 * by
+    wide = by + 2
+    packed = order // 2 + order // 8
+    copies = 2 * bx + 2 + 2 * by
     gram, sums = pl.pallas_call(
         gram_kernel,
-        out_shape=(pltpu.VMEM((bx, by, order, order), f32), jax.ShapeDtypeStruct((9, bx * by), f32)),
-        in_specs=[anyspace, vmem, vmem, smem, smem, smem],
-        out_specs=(vmem, smem),
+        out_shape=(pltpu.VMEM((bx, by, order, order), f32), pltpu.VMEM((9, bx, by, order), f32)),
+        in_specs=[anyspace] * 6,
+        out_specs=(vmem, vmem),
         scratch_shapes=[
-            pltpu.VMEM((padded, coupling, order), bf16),
-            pltpu.VMEM((padded, order, coupling), bf16),
-            pltpu.SemaphoreType.DMA((bx,)),
+            pltpu.VMEM((bx * wide, coupling, order), bf16),
+            pltpu.VMEM((bx * wide, order, coupling), bf16),
+            pltpu.VMEM(permit.shape, f32), pltpu.VMEM(shift_diag.shape, f32),
+            pltpu.VMEM(codes.shape, jnp.int32), pltpu.VMEM(counts.shape, jnp.int32), pltpu.VMEM(weights.shape, f32),
+            pltpu.VMEM((order, order), f32),
+            pltpu.VMEM((bx, 9, by, coupling), f32), pltpu.VMEM((2, 3, by, coupling), f32),
+            pltpu.VMEM((2, by, packed, order), f32), pltpu.VMEM((2, by, packed, order), f32),
+            pltpu.SemaphoreType.DMA((bx,)), pltpu.SemaphoreType.DMA((5,)),
             pltpu.SemaphoreType.DMA((copies,)), pltpu.SemaphoreType.DMA((copies,)),
         ],
         compiler_params=pltpu.CompilerParams(collective_id=0, has_side_effects=True),
@@ -414,7 +431,7 @@
     applied = pl.pallas_call(
         sum_kernel,
         out_shape=pltpu.VMEM((bx, by, order, nv), bf16),
-        in_specs=[vmem, vmem, smem],
+        in_specs=[vmem, vmem, vmem],
         out_specs=vmem,
         scratch_shapes=[
             pltpu.VMEM((bx, by, order, nv), f32),
@@ -424,7 +441,7 @@
         ],
         compiler_params=pltpu.CompilerParams(collective_id=1, has_side_effects=True),
         name="sums",
-    )(pltpu.with_memory_space_constraint(held, pltpu.VMEM), vectors, sums)
+    )(pltpu.with_memory_space_constraint(held, pltpu.VMEM), vectors, pltpu.with_memory_space_constraint(sums, pltpu.VMEM))
     return fac, applied
 
 

time: 45.6 us -> 39.3 us (0.86)
  the two profiles are of different devices: /device:TPU:4 before, /device:TPU:0 now
where the time goes in v2:
time: 39.3 us; the launch traced here: 39.1 us
  Pallas kernels  37.6 us (96%)
  local copies, waits for them, and re-layouts  0.8 us (2%)
  between operations  0.66 us (2%)
    pallas_call x1, Pallas kernels, local(): pl.pallas_call(gram_kernel, out_shape=(pltpu.VMEM((bx, by, order, order),...  15.9 us
    pallas_call x1, Pallas kernels, local(): pl.pallas_call(sum_kernel, out_shape=pltpu.VMEM((bx, by, order, nv), bf16...  12.5 us
    pallas_call x1, Pallas kernels, local(): pl.pallas_call(factor_kernel, out_shape=(jax.ShapeDtypeStruct((bx, by, or...  9.14 us
    unnamed x1, local copies, waits for them, and re-layouts  0.8 us

profile of v2, /device:TPU:0, one launch (start us, length us, event | category | flops | bytes accessed | tf_op | source)
XLA Modules:
  0.0 39.1 jit_solution(16546777290446352968)
XLA Ops:
  0.6 15.9 %gram.1 = (f32[2,8,128,128]{3,2,1,0:T(8,128)S(1)}, f32[9,2,8,128]{3,2,1,0:T(8,128)S(1)}) custom-call(bf16[2,8,256,128]{3,2,1,0:T(8,128)(2,1)} %c_ref.1, f32[2,8,256]{2,1,0:T(8,128)} %permit_ref.1, f32[2,8,128]{2,1,0:T(8,128)} %shift_ref.1, s32[6,2,8]{2,1,0:T(2,128)} %bitcast.2, s32[2,8]{1,0:T(2,128)} %counts_ref.1, f32[6,2,8]{2,1,0:T(2,128)} %bitcast.3), custom_call_target="tpu_custom_call" | custom-call | tf_op jit(solution)/shard_map/gram/pallas_call | solution.py:399
  16.6 9.1 %factor.1 = (bf16[2,8,128,128]{3,2,1,0:T(8,128)(2,1)}, bf16[2,8,128,128]{3,2,1,0:T(8,128)(2,1)S(1)}) custom-call(f32[2,8,128,128]{3,2,1,0:T(8,128)S(1)} %get-tuple-element.6.gram_ref), custom_call_target="tpu_custom_call" | custom-call | tf_op jit(solution)/shard_map/factor/pallas_call | solution.py:418
  25.7 12.5 %sums.1 = bf16[2,8,128,128]{3,2,1,0:T(8,128)(2,1)S(1)} custom-call(bf16[2,8,128,128]{3,2,1,0:T(8,128)(2,1)S(1)} %get-tuple-element.8.fac_ref, bf16[2,8,128,128]{3,2,1,0:T(8,128)(2,1)} %v_ref.1, f32[9,2,8,128]{3,2,1,0:T(8,128)S(1)} %get-tuple-element.9.wt), custom_call_target="tpu_custom_call" | custom-call | tf_op jit(solution)/shard_map/sums/pallas_call | solution.py:431
  38.3 0.8 %copy.10 = bf16[2,8,128,128]{3,2,1,0:T(8,128)(2,1)} copy(bf16[2,8,128,128]{3,2,1,0:T(8,128)(2,1)S(1)} %sums.1) | data formatting | bytes 1048576

commit v3 on v2

--- a/solution.py
+++ b/solution.py
@@ -226,18 +226,25 @@
     return h, (x - h.astype(jnp.float32)).astype(jnp.bfloat16)
 
 
-def factor_kernel(gram_ref, out_ref, fac_ref, gs, sem):
+def factor_kernel(gram_ref, v_ref, out_ref, fac_ref, held_ref, gs, v_sem, sem):
     bx, by, order = gram_ref.shape[:3]
     blocks = bx * by
+    fetch = pltpu.make_async_copy(v_ref, held_ref, v_sem)
+    fetch.start()
     for i in range(blocks):
         gs[i] = gram_ref[i // by, i % by]
-    factor(gs, fac_ref, bx, by, order)
-    copy = pltpu.make_async_copy(fac_ref, out_ref, sem)
-    copy.start()
-    copy.wait()
-
-
-def factor(gs, fac_ref, bx, by, order):
+
+    def put(stage):
+        rows = pl.ds(stage * BASE, BASE)
+        return pltpu.make_async_copy(fac_ref.at[:, :, rows], out_ref.at[:, :, rows], sem.at[stage])
+
+    factor(gs, fac_ref, bx, by, order, put)
+    for stage in range(order // BASE):
+        put(stage).wait()
+    fetch.wait()
+
+
+def factor(gs, fac_ref, bx, by, order, put):
     blocks = bx * by
     lanes = lax.broadcasted_iota(jnp.int32, (order, order), 1)
     per = order // BASE
@@ -306,28 +313,33 @@
                     below = gs[at, high:, :]
                     below = jnp.where(lanes[high:] // BASE == stage, 0.0, below)
                     gs[at, high:, :] = below - update
-
-
-def sum_kernel(fac_ref, v_ref, wt, out_ref, img, loc, px, py, pc, rx, ry, rc, send_sem, recv_sem):
+        put(stage).start()
+
+
+def sum_kernel(fac_ref, v_ref, wt, out_ref, img, loc, px, py, rx, ry, send_sem, recv_sem):
     bx, by = fac_ref.shape[:2]
     there, exists = neighbours()
-    sends = [px.at[0], px.at[1], py.at[0], py.at[1]] + [pc.at[k] for k in range(4)]
-    lands = [rx.at[0], rx.at[1], ry.at[0], ry.at[1]] + [rc.at[k] for k in range(4)]
+    gx_dirs, gy_dirs = DIRS[:2], DIRS[2:4]
     barrier = pltpu.get_barrier_semaphore()
-    for d in DIRS:
+    for d in DIRS[:4]:
         @pl.when(exists(d))
         def _(d=d):
             pl.semaphore_signal(barrier, inc=1, device_id=there(d), device_id_type=MESH)
-    for k, d in enumerate(DIRS):
-        @pl.when(jnp.logical_not(exists((-d[0], -d[1]))))
-        def _(k=k):
-            lands[k][...] = jnp.zeros(lands[k].shape, lands[k].dtype)
-
-    @pl.loop(0, by)
-    def _(y):
-        for x in range(bx):
-            img[x, y] = lax.dot_general(fac_ref[x, y], v_ref[x, y], (((0,), (0,)), ((), ())),
-                                        preferred_element_type=jnp.float32)
+
+    def remote(source, target, k, d):
+        return pltpu.make_async_remote_copy(
+            src_ref=source, dst_ref=target, send_sem=send_sem.at[k], recv_sem=recv_sem.at[k],
+            device_id=there(d), device_id_type=MESH)
+
+    def gx_copy(k, y):
+        return remote(px.at[k, y], rx.at[k, y], k * by + y, gx_dirs[k])
+
+    def gy_copy(k, x):
+        return remote(py.at[k, x], ry.at[k, x], 2 * by + k * (bx + 2) + x, gy_dirs[k])
+
+    def image(x, y):
+        img[x, y] = lax.dot_general(fac_ref[x, y], v_ref[x, y], (((0,), (0,)), ((), ())),
+                                    preferred_element_type=jnp.float32)
 
     def target(tx, ty):
         total = None
@@ -339,51 +351,101 @@
                     total = term if total is None else total + term
         return total
 
-    for y in range(by):
-        px[0, y] = target(bx + 1, y + 1).astype(px.dtype)
-        px[1, y] = target(0, y + 1).astype(px.dtype)
-    for k, d in enumerate(DIRS[4:]):
-        pc[k] = target(bx + 1 if d[0] > 0 else 0, by + 1 if d[1] > 0 else 0).astype(pc.dtype)
+    rows = (bx + 1, 0)
+    edges = (by - 1, 0)
+    ends = sorted({0, by - 1})
+    for y in ends:
+        for x in range(bx):
+            image(x, y)
+    for k in range(2):
+        for r in rows:
+            py[k, r] = target(r, (by + 1, 0)[k]).astype(py.dtype)
+    near = [exists(d).astype(jnp.int32) for d in DIRS[:4]]
+    pl.semaphore_wait(barrier, near[0] + near[1] + near[2] + near[3])
+    for k, d in enumerate(gy_dirs):
+        @pl.when(exists(d))
+        def _(k=k):
+            for r in rows:
+                gy_copy(k, r).start()
+
+        @pl.when(jnp.logical_not(exists((-d[0], -d[1]))))
+        def _(k=k):
+            ry[k] = jnp.zeros(ry.shape[1:], ry.dtype)
+    for k, d in enumerate(gx_dirs):
+        @pl.when(jnp.logical_not(exists((-d[0], -d[1]))))
+        def _(k=k):
+            rx[k] = jnp.zeros(rx.shape[1:], rx.dtype)
+    ready = set(ends)
+    for y in range(1, by - 1):
+        for n in (y - 1, y, y + 1):
+            if n not in ready:
+                ready.add(n)
+                for x in range(bx):
+                    image(x, n)
+        for k, d in enumerate(gx_dirs):
+            px[k, y] = target(rows[k], y + 1).astype(px.dtype)
+        for k, d in enumerate(gx_dirs):
+            @pl.when(exists(d))
+            def _(k=k, y=y):
+                gx_copy(k, y).start()
+    for k in range(2):
+        for x in range(1, bx + 1):
+            py[k, x] = target(x, (by + 1, 0)[k]).astype(py.dtype)
+    for k, d in enumerate(gy_dirs):
+        @pl.when(exists(d))
+        def _(k=k):
+            for x in range(1, bx + 1):
+                gy_copy(k, x).start()
+    for y in ends:
+        for x in range(bx):
+            loc[x, y] = target(x + 1, y + 1)
+    for k, d in enumerate(gy_dirs):
+        @pl.when(exists((-d[0], -d[1])))
+        def _(k=k):
+            for r in rows:
+                gy_copy(k, r).wait_recv()
+    for y in ends:
+        for k in range(2):
+            total = target(rows[k], y + 1)
+            for j in range(2):
+                if y == edges[1 - j]:
+                    total = total + ry[j, rows[k]].astype(jnp.float32)
+            px[k, y] = total.astype(px.dtype)
+        for k, d in enumerate(gx_dirs):
+            @pl.when(exists(d))
+            def _(k=k, y=y):
+                gx_copy(k, y).start()
     for x in range(bx):
-        py[0, x] = target(x + 1, by + 1).astype(py.dtype)
-        py[1, x] = target(x + 1, 0).astype(py.dtype)
-    near = [exists(d).astype(jnp.int32) for d in DIRS[:4]]
-    pl.semaphore_wait(barrier, (near[0] + near[1] + 1) * (near[2] + near[3] + 1) - 1)
-
-    def copy(k, d):
-        return pltpu.make_async_remote_copy(
-            src_ref=sends[k], dst_ref=lands[k], send_sem=send_sem.at[k], recv_sem=recv_sem.at[k],
-            device_id=there(d), device_id_type=MESH)
-
-    order_of = (4, 5, 6, 7, 0, 1, 2, 3)
-    for k in order_of:
-        @pl.when(exists(DIRS[k]))
-        def _(k=k):
-            copy(k, DIRS[k]).start()
-    for x in range(bx):
-        for y in range(by):
+        for y in range(1, by - 1):
             loc[x, y] = target(x + 1, y + 1)
-    for k in order_of:
-        @pl.when(exists((-DIRS[k][0], -DIRS[k][1])))
-        def _(k=k):
-            copy(k, DIRS[k]).wait_recv()
-    for x in range(bx):
-        for y in range(by):
+    for k, d in enumerate(gy_dirs):
+        @pl.when(exists((-d[0], -d[1])))
+        def _(k=k):
+            for x in range(1, bx + 1):
+                gy_copy(k, x).wait_recv()
+    for y in list(range(1, by - 1)) + ends:
+        for k, d in enumerate(gx_dirs):
+            @pl.when(exists((-d[0], -d[1])))
+            def _(k=k, y=y):
+                gx_copy(k, y).wait_recv()
+        for x in range(bx):
             total = loc[x, y]
-            for k, edge in ((0, 0), (1, bx - 1)):
-                if x == edge:
+            for k in range(2):
+                if x == (0, bx - 1)[k]:
                     total = total + rx[k, y].astype(jnp.float32)
-            for k, edge in ((0, 0), (1, by - 1)):
-                if y == edge:
-                    total = total + ry[k, x].astype(jnp.float32)
-            for k, place in enumerate(((0, 0), (0, by - 1), (bx - 1, 0), (bx - 1, by - 1))):
-                if (x, y) == place:
-                    total = total + rc[k].astype(jnp.float32)
+                if y == edges[1 - k]:
+                    total = total + ry[k, x + 1].astype(jnp.float32)
             out_ref[x, y] = total.astype(out_ref.dtype)
-    for k in order_of:
-        @pl.when(exists(DIRS[k]))
-        def _(k=k):
-            copy(k, DIRS[k]).wait_send()
+    for k, d in enumerate(gx_dirs):
+        @pl.when(exists(d))
+        def _(k=k):
+            for y in range(by):
+                gx_copy(k, y).wait_send()
+    for k, d in enumerate(gy_dirs):
+        @pl.when(exists(d))
+        def _(k=k):
+            for x in range(bx + 2):
+                gy_copy(k, x).wait_send()
 
 
 def local(coeffs, permit, shift_diag, codes, counts, weights, vectors):
@@ -415,19 +477,23 @@
         compiler_params=pltpu.CompilerParams(collective_id=0, has_side_effects=True),
         name="gram",
     )(coeffs, permit, shift_diag, codes, counts, weights)
-    fac, held = pl.pallas_call(
+    fac, held, vecs = pl.pallas_call(
         factor_kernel,
-        out_shape=(jax.ShapeDtypeStruct((bx, by, order, order), bf16), pltpu.VMEM((bx, by, order, order), bf16)),
-        in_specs=[vmem],
-        out_specs=(anyspace, vmem),
-        scratch_shapes=[pltpu.VMEM((bx * by, order, order), f32), pltpu.SemaphoreType.DMA],
+        out_shape=(
+            jax.ShapeDtypeStruct((bx, by, order, order), bf16),
+            pltpu.VMEM((bx, by, order, order), bf16),
+            pltpu.VMEM((bx, by, order, nv), bf16),
+        ),
+        in_specs=[vmem, anyspace],
+        out_specs=(anyspace, vmem, vmem),
+        scratch_shapes=[
+            pltpu.VMEM((bx * by, order, order), f32), pltpu.SemaphoreType.DMA,
+            pltpu.SemaphoreType.DMA((order // BASE,)),
+        ],
         name="factor",
-    )(pltpu.with_memory_space_constraint(gram, pltpu.VMEM))
-    edges = [
-        pltpu.VMEM((2, by, order, nv), bf16),
-        pltpu.VMEM((2, bx, order, nv), bf16),
-        pltpu.VMEM((4, order, nv), bf16),
-    ]
+    )(pltpu.with_memory_space_constraint(gram, pltpu.VMEM), vectors)
+    edges = [pltpu.VMEM((2, by, order, nv), bf16), pltpu.VMEM((2, bx + 2, order, nv), bf16)]
+    copies = 2 * by + 2 * (bx + 2)
     applied = pl.pallas_call(
         sum_kernel,
         out_shape=pltpu.VMEM((bx, by, order, nv), bf16),
@@ -437,11 +503,11 @@
             pltpu.VMEM((bx, by, order, nv), f32),
             pltpu.VMEM((bx, by, order, nv), f32),
             *edges, *edges,
-            pltpu.SemaphoreType.DMA((8,)), pltpu.SemaphoreType.DMA((8,)),
+            pltpu.SemaphoreType.DMA((copies,)), pltpu.SemaphoreType.DMA((copies,)),
         ],
         compiler_params=pltpu.CompilerParams(collective_id=1, has_side_effects=True),
         name="sums",
-    )(pltpu.with_memory_space_constraint(held, pltpu.VMEM), vectors, pltpu.with_memory_space_constraint(sums, pltpu.VMEM))
+    )(*(pltpu.with_memory_space_constraint(x, pltpu.VMEM) for x in (held, vecs, sums)))
     return fac, applied
 
 

time: 39.3 us -> 36.6 us (0.931)
  Pallas kernels: 37.6 us -> 35 us
    pallas_call x1, Pallas kernels: 12.5 us -> 9.98 us  [local(): pl.pallas_call(sum_kernel, out_shape=pltpu.VMEM((bx, by, order, nv), bf16...]
where the time goes in v3:
time: 36.6 us; the launch traced here: 36.4 us
  Pallas kernels  35 us (96%)
  local copies, waits for them, and re-layouts  0.8 us (2%)
  between operations  0.66 us (2%)
    pallas_call x1, Pallas kernels, local(): pl.pallas_call(gram_kernel, out_shape=(pltpu.VMEM((bx, by, order, order),...  15.9 us
    pallas_call x1, Pallas kernels, local(): pl.pallas_call(sum_kernel, out_shape=pltpu.VMEM((bx, by, order, nv), bf16...  9.98 us
    pallas_call x1, Pallas kernels, local(): pl.pallas_call(factor_kernel, out_shape=(jax.ShapeDtypeStruct((bx, by, or...  9.05 us
    unnamed x1, local copies, waits for them, and re-layouts  0.8 us

profile of v3, /device:TPU:0, one launch (start us, length us, event | category | flops | bytes accessed | tf_op | source)
XLA Modules:
  0.0 36.4 jit_solution(12482227758300574287)
XLA Ops:
  0.6 15.9 %gram.1 = (f32[2,8,128,128]{3,2,1,0:T(8,128)S(1)}, f32[9,2,8,128]{3,2,1,0:T(8,128)S(1)}) custom-call(bf16[2,8,256,128]{3,2,1,0:T(8,128)(2,1)} %c_ref.1, f32[2,8,256]{2,1,0:T(8,128)} %permit_ref.1, f32[2,8,128]{2,1,0:T(8,128)} %shift_ref.1, s32[6,2,8]{2,1,0:T(2,128)} %bitcast.2, s32[2,8]{1,0:T(2,128)} %counts_ref.1, f32[6,2,8]{2,1,0:T(2,128)} %bitcast.3), custom_call_target="tpu_custom_call" | custom-call | tf_op jit(solution)/shard_map/gram/pallas_call | solution.py:461
  16.6 9.0 %factor.1 = (bf16[2,8,128,128]{3,2,1,0:T(8,128)(2,1)}, bf16[2,8,128,128]{3,2,1,0:T(8,128)(2,1)S(1)}, bf16[2,8,128,128]{3,2,1,0:T(8,128)(2,1)S(1)}) custom-call(f32[2,8,128,128]{3,2,1,0:T(8,128)S(1)} %get-tuple-element.7.gram_ref, bf16[2,8,128,128]{3,2,1,0:T(8,128)(2,1)} %v_ref.1), custom_call_target="tpu_custom_call" | custom-call | tf_op jit(solution)/shard_map/factor/pallas_call | solution.py:480
  25.6 10.0 %sums.1 = bf16[2,8,128,128]{3,2,1,0:T(8,128)(2,1)S(1)} custom-call(bf16[2,8,128,128]{3,2,1,0:T(8,128)(2,1)S(1)} %get-tuple-element.9.fac_ref, bf16[2,8,128,128]{3,2,1,0:T(8,128)(2,1)S(1)} %get-tuple-element.10.v_ref, f32[9,2,8,128]{3,2,1,0:T(8,128)S(1)} %get-tuple-element.11.wt), custom_call_target="tpu_custom_call" | custom-call | tf_op jit(solution)/shard_map/sums/pallas_call | solution.py:497
  35.6 0.8 %copy.10 = bf16[2,8,128,128]{3,2,1,0:T(8,128)(2,1)} copy(bf16[2,8,128,128]{3,2,1,0:T(8,128)(2,1)S(1)} %sums.1) | data formatting | bytes 1048576

commit v4 on v3

--- a/solution.py
+++ b/solution.py
@@ -116,25 +116,32 @@
     def turn(n):
         ts[n] = cs[n].T
 
+    def scaled(n, scale):
+        rows = jnp.broadcast_to(scale, (16, coupling)).astype(jnp.bfloat16)
+        return (ts[n].reshape(order // 16, 16, coupling) * rows[None]).reshape(order, coupling)
+
     def terms(r, y, scales):
-        left = jnp.concatenate([(ts[r * wide + y + ay].astype(jnp.float32) * scales(ay)).astype(jnp.bfloat16)
-                                for ay in range(3)], axis=1)
+        left = jnp.concatenate([
+            jnp.concatenate([scaled(r * wide + y + ay, scale(ay)) for ay in range(3)], axis=1) for scale in scales], axis=0)
         right = cs[pl.ds(r * wide + y, 3)].reshape(3 * coupling, order)
         return jnp.dot(left, right, preferred_element_type=jnp.float32)
 
     same = lax.broadcasted_iota(jnp.int32, (order, order), 0) == lax.broadcasted_iota(jnp.int32, (order, order), 1)
 
     def inner(y):
+        accs = [jnp.where(same, sh[x, pl.ds(y, 1), :], 0.0) for x in range(bx)]
+        for r in range(bx):
+            targets = range(max(0, r - 1), min(bx, r + 2))
+            out = terms(r, y, [lambda ay, x=x: tp[x, (r - x + 1) * 3 + ay, pl.ds(y, 1), :] for x in targets])
+            for k, x in enumerate(targets):
+                accs[x] = accs[x] + out[k * order:(k + 1) * order]
         for x in range(bx):
-            acc = jnp.where(same, sh[x, pl.ds(y, 1), :], 0.0)
-            for r in range(max(0, x - 1), min(bx, x + 2)):
-                acc = acc + terms(r, y, lambda ay: tp[x, (r - x + 1) * 3 + ay, pl.ds(y, 1), :])
-            gram_ref[x, y] = acc
+            gram_ref[x, y] = accs[x]
 
     lane = lax.broadcasted_iota(jnp.int32, (quarter, order), 1)
 
     def outer(j, y):
-        acc = terms((0, bx - 1)[j], y, lambda ay: tq[j, ay, pl.ds(y, 1), :])
+        acc = terms((0, bx - 1)[j], y, [lambda ay: tq[j, ay, pl.ds(y, 1), :]])
         ps[j, y, 0:quarter] = acc[0:quarter]
         ps[j, y, quarter:2 * quarter] = jnp.where(
             lane < quarter, pltpu.roll(acc[3 * quarter:], quarter, axis=1), acc[quarter:2 * quarter])
@@ -142,10 +149,12 @@
         ps[j, y, 2 * quarter:mid] = jnp.where(
             lane[:quarter // 2] < 2 * quarter, pltpu.roll(acc[mid:3 * quarter], 2 * quarter, axis=1), acc[2 * quarter:mid])
 
-    def send(j, y):
-        @pl.when(exists(gx_dirs[1 - j]))
-        def _():
-            part_copy(j, y).start()
+    def send(ys):
+        for j in range(2):
+            @pl.when(exists(gx_dirs[1 - j]))
+            def _(j=j):
+                for y in ys:
+                    part_copy(j, y).start()
 
     for copy in own:
         copy.wait()
@@ -156,19 +165,20 @@
             turn(x * wide + y + 1)
     split_at = by // 2
 
-    @pl.loop(1, split_at)
-    def _(y):
+    for y in range(1, split_at):
         inner(y)
 
     for j in range(2):
         @pl.when(exists(gx_dirs[1 - j]))
         def _(j=j):
             scale_copy(j).wait_recv()
-    for y in range(1, by - 1):
-        for j in range(2):
-            outer(j, y)
-        for j in range(2):
-            send(j, y)
+    chunk = 3
+    for low in range(1, by - 1, chunk):
+        ys = range(low, min(low + chunk, by - 1))
+        for y in ys:
+            for j in range(2):
+                outer(j, y)
+        send(ys)
     for j, d in enumerate(gy_dirs):
         @pl.when(exists((-d[0], -d[1])))
         def _(j=j):
@@ -177,19 +187,13 @@
     for x in range(bx):
         turn(x * wide)
         turn(x * wide + by + 1)
-    for y in sorted({0, by - 1}):
+    ends = sorted({0, by - 1})
+    for y in ends:
         for j in range(2):
             outer(j, y)
-        for j in range(2):
-            send(j, y)
-
-    @pl.loop(split_at, by - 1)
-    def _(y):
+    send(ends)
+    for y in list(range(split_at, by - 1)) + ends:
         inner(y)
-
-    @pl.loop(0, 2)
-    def _(e):
-        inner(e * (by - 1))
 
     mid = 2 * quarter + quarter // 2
     for y in list(range(1, by - 1)) + sorted({0, by - 1}):

time: 36.6 us -> 36.4 us (level)
    pallas_call x1, Pallas kernels: 9.98 us -> 9.55 us  [local(): pl.pallas_call(sum_kernel, out_shape=pltpu.VMEM((bx, by, order, nv), bf16...]
where the time goes in v4:
time: 36.4 us; the launch traced here: 36.2 us
  Pallas kernels  34.7 us (95%)
  local copies, waits for them, and re-layouts  0.8 us (2%)
  between operations  0.66 us (2%)
    pallas_call x1, Pallas kernels, local(): pl.pallas_call(gram_kernel, out_shape=(pltpu.VMEM((bx, by, order, order),...  16.1 us
    pallas_call x1, Pallas kernels, local(): pl.pallas_call(sum_kernel, out_shape=pltpu.VMEM((bx, by, order, nv), bf16...  9.55 us
    pallas_call x1, Pallas kernels, local(): pl.pallas_call(factor_kernel, out_shape=(jax.ShapeDtypeStruct((bx, by, or...  9.04 us
    unnamed x1, local copies, waits for them, and re-layouts  0.8 us

profile of v4, /device:TPU:0, one launch (start us, length us, event | category | flops | bytes accessed | tf_op | source)
XLA Modules:
  0.0 36.2 jit_solution(9643088548991879247)
XLA Ops:
  0.6 16.1 %gram.1 = (f32[2,8,128,128]{3,2,1,0:T(8,128)S(1)}, f32[9,2,8,128]{3,2,1,0:T(8,128)S(1)}) custom-call(bf16[2,8,256,128]{3,2,1,0:T(8,128)(2,1)} %c_ref.1, f32[2,8,256]{2,1,0:T(8,128)} %permit_ref.1, f32[2,8,128]{2,1,0:T(8,128)} %shift_ref.1, s32[6,2,8]{2,1,0:T(2,128)} %bitcast.2, s32[2,8]{1,0:T(2,128)} %counts_ref.1, f32[6,2,8]{2,1,0:T(2,128)} %bitcast.3), custom_call_target="tpu_custom_call" | custom-call | tf_op jit(solution)/shard_map/gram/pallas_call | solution.py:465
  16.8 9.0 %factor.1 = (bf16[2,8,128,128]{3,2,1,0:T(8,128)(2,1)}, bf16[2,8,128,128]{3,2,1,0:T(8,128)(2,1)S(1)}, bf16[2,8,128,128]{3,2,1,0:T(8,128)(2,1)S(1)}) custom-call(f32[2,8,128,128]{3,2,1,0:T(8,128)S(1)} %get-tuple-element.7.gram_ref, bf16[2,8,128,128]{3,2,1,0:T(8,128)(2,1)} %v_ref.1), custom_call_target="tpu_custom_call" | custom-call | tf_op jit(solution)/shard_map/factor/pallas_call | solution.py:484
  25.8 9.5 %sums.1 = bf16[2,8,128,128]{3,2,1,0:T(8,128)(2,1)S(1)} custom-call(bf16[2,8,128,128]{3,2,1,0:T(8,128)(2,1)S(1)} %get-tuple-element.9.fac_ref, bf16[2,8,128,128]{3,2,1,0:T(8,128)(2,1)S(1)} %get-tuple-element.10.v_ref, f32[9,2,8,128]{3,2,1,0:T(8,128)S(1)} %get-tuple-element.11.wt), custom_call_target="tpu_custom_call" | custom-call | tf_op jit(solution)/shard_map/sums/pallas_call | solution.py:501
  35.4 0.8 %copy.10 = bf16[2,8,128,128]{3,2,1,0:T(8,128)(2,1)} copy(bf16[2,8,128,128]{3,2,1,0:T(8,128)(2,1)S(1)} %sums.1) | data formatting | bytes 1048576

commit v5 on v4

--- a/solution.py
+++ b/solution.py
@@ -88,12 +88,13 @@
     def column(c):
         return jnp.take_along_axis(turned, jnp.full((by, order), c, jnp.int32), axis=1)
 
-    for o in (6, 7, 8, 0, 1, 2, 3, 4, 5):
-        for x in range(bx):
-            times = column(o * bx + x)
-            tp[x, o] = pm[x] * jnp.concatenate([times] * (coupling // order), axis=1)
-            wrow_ref[o, x] = column(half + o * bx + x)
-
+    def spread(x, o):
+        times = column(o * bx + x)
+        tp[x, o] = pm[x] * jnp.concatenate([times] * (coupling // order), axis=1)
+
+    sent = [(bx - 1, o) for o in range(6, 9)] + [(0, o) for o in range(3)]
+    for x, o in sent:
+        spread(x, o)
     near = [exists(d).astype(jnp.int32) for d in DIRS[:4]]
     pl.semaphore_wait(barrier, near[0] + near[1] + near[2] + near[3])
     for j, d in enumerate(gx_dirs):
@@ -106,6 +107,11 @@
             for x in range(bx):
                 gy_copy(j, x).start()
 
+    for o in range(9):
+        for x in range(bx):
+            if (x, o) not in sent:
+                spread(x, o)
+            wrow_ref[o, x] = column(half + o * bx + x)
     zero = jnp.zeros((coupling, order), cs.dtype)
     for j, d in enumerate(gy_dirs):
         @pl.when(jnp.logical_not(exists((-d[0], -d[1]))))
@@ -163,16 +169,12 @@
         @pl.loop(0, by, unroll=2)
         def _(y):
             turn(x * wide + y + 1)
-    split_at = by // 2
-
-    for y in range(1, split_at):
-        inner(y)
 
     for j in range(2):
         @pl.when(exists(gx_dirs[1 - j]))
         def _(j=j):
             scale_copy(j).wait_recv()
-    chunk = 3
+    chunk = 2
     for low in range(1, by - 1, chunk):
         ys = range(low, min(low + chunk, by - 1))
         for y in ys:
@@ -192,7 +194,7 @@
         for j in range(2):
             outer(j, y)
     send(ends)
-    for y in list(range(split_at, by - 1)) + ends:
+    for y in list(range(1, by - 1)) + ends:
         inner(y)
 
     mid = 2 * quarter + quarter // 2

time: 36.4 us -> 36.4 us (level)
  no operation moved by 1% of the time
where the time goes in v5:
time: 36.4 us; the launch traced here: 36.2 us
  Pallas kernels  34.7 us (95%)
  local copies, waits for them, and re-layouts  0.8 us (2%)
  between operations  0.66 us (2%)
    pallas_call x1, Pallas kernels, local(): pl.pallas_call(gram_kernel, out_shape=(pltpu.VMEM((bx, by, order, order),...  16.1 us
    pallas_call x1, Pallas kernels, local(): pl.pallas_call(sum_kernel, out_shape=pltpu.VMEM((bx, by, order, nv), bf16...  9.63 us
    pallas_call x1, Pallas kernels, local(): pl.pallas_call(factor_kernel, out_shape=(jax.ShapeDtypeStruct((bx, by, or...  9.04 us
    unnamed x1, local copies, waits for them, and re-layouts  0.8 us

profile of v5, /device:TPU:0, one launch (start us, length us, event | category | flops | bytes accessed | tf_op | source)
XLA Modules:
  0.0 36.2 jit_solution(6104615456790437638)
XLA Ops:
  0.6 16.1 %gram.1 = (f32[2,8,128,128]{3,2,1,0:T(8,128)S(1)}, f32[9,2,8,128]{3,2,1,0:T(8,128)S(1)}) custom-call(bf16[2,8,256,128]{3,2,1,0:T(8,128)(2,1)} %c_ref.1, f32[2,8,256]{2,1,0:T(8,128)} %permit_ref.1, f32[2,8,128]{2,1,0:T(8,128)} %shift_ref.1, s32[6,2,8]{2,1,0:T(2,128)} %bitcast.2, s32[2,8]{1,0:T(2,128)} %counts_ref.1, f32[6,2,8]{2,1,0:T(2,128)} %bitcast.3), custom_call_target="tpu_custom_call" | custom-call | tf_op jit(solution)/shard_map/gram/pallas_call | solution.py:467
  16.7 9.0 %factor.1 = (bf16[2,8,128,128]{3,2,1,0:T(8,128)(2,1)}, bf16[2,8,128,128]{3,2,1,0:T(8,128)(2,1)S(1)}, bf16[2,8,128,128]{3,2,1,0:T(8,128)(2,1)S(1)}) custom-call(f32[2,8,128,128]{3,2,1,0:T(8,128)S(1)} %get-tuple-element.7.gram_ref, bf16[2,8,128,128]{3,2,1,0:T(8,128)(2,1)} %v_ref.1), custom_call_target="tpu_custom_call" | custom-call | tf_op jit(solution)/shard_map/factor/pallas_call | solution.py:486
  25.7 9.6 %sums.1 = bf16[2,8,128,128]{3,2,1,0:T(8,128)(2,1)S(1)} custom-call(bf16[2,8,128,128]{3,2,1,0:T(8,128)(2,1)S(1)} %get-tuple-element.9.fac_ref, bf16[2,8,128,128]{3,2,1,0:T(8,128)(2,1)S(1)} %get-tuple-element.10.v_ref, f32[9,2,8,128]{3,2,1,0:T(8,128)S(1)} %get-tuple-element.11.wt), custom_call_target="tpu_custom_call" | custom-call | tf_op jit(solution)/shard_map/sums/pallas_call | solution.py:503
  35.4 0.8 %copy.10 = bf16[2,8,128,128]{3,2,1,0:T(8,128)(2,1)} copy(bf16[2,8,128,128]{3,2,1,0:T(8,128)(2,1)S(1)} %sums.1) | data formatting | bytes 1048576

commit v6 on v5

--- a/solution.py
+++ b/solution.py
@@ -33,7 +33,7 @@
 
 
 def gram_kernel(c_ref, permit_ref, shift_ref, codes_ref, counts_ref, weights_ref, gram_ref, wrow_ref,
-                cs, ts, pm, sh, cd, ct, wg, flat, tp, tq, ps, pr, own_sem, in_sem, send_sem, recv_sem):
+                cs, ts, pm, sh, cd, ct, wg, flat, tp, tb, tq, ps, pr, own_sem, in_sem, send_sem, recv_sem):
     bx, by, coupling, order = c_ref.shape
     slots = codes_ref.shape[0]
     wide = by + 2
@@ -64,8 +64,7 @@
         return remote(c_ref.at[x, edge[d[1]]], cs.at[x * wide + land[d[1]]], j * bx + x, d)
 
     def scale_copy(j):
-        x, o = ((bx - 1, 6), (0, 0))[j]
-        return remote(tp.at[x, pl.ds(o, 3)], tq.at[j], 2 * bx + j, gx_dirs[j])
+        return remote(tb.at[j], tq.at[j], 2 * bx + j, gx_dirs[j])
 
     def part_copy(j, y):
         return remote(ps.at[j, y], pr.at[j, y], 2 * bx + 2 + j * by + y, gx_dirs[1 - j])
@@ -93,8 +92,9 @@
         tp[x, o] = pm[x] * jnp.concatenate([times] * (coupling // order), axis=1)
 
     sent = [(bx - 1, o) for o in range(6, 9)] + [(0, o) for o in range(3)]
-    for x, o in sent:
+    for n, (x, o) in enumerate(sent):
         spread(x, o)
+        tb[n // 3, n % 3] = tp[x, o].astype(tb.dtype)
     near = [exists(d).astype(jnp.int32) for d in DIRS[:4]]
     pl.semaphore_wait(barrier, near[0] + near[1] + near[2] + near[3])
     for j, d in enumerate(gx_dirs):
@@ -147,7 +147,7 @@
     lane = lax.broadcasted_iota(jnp.int32, (quarter, order), 1)
 
     def outer(j, y):
-        acc = terms((0, bx - 1)[j], y, [lambda ay: tq[j, ay, pl.ds(y, 1), :]])
+        acc = terms((0, bx - 1)[j], y, [lambda ay: tq[j, ay].astype(jnp.float32)[y:y + 1]])
         ps[j, y, 0:quarter] = acc[0:quarter]
         ps[j, y, quarter:2 * quarter] = jnp.where(
             lane < quarter, pltpu.roll(acc[3 * quarter:], quarter, axis=1), acc[quarter:2 * quarter])
@@ -174,9 +174,10 @@
         @pl.when(exists(gx_dirs[1 - j]))
         def _(j=j):
             scale_copy(j).wait_recv()
-    chunk = 2
-    for low in range(1, by - 1, chunk):
-        ys = range(low, min(low + chunk, by - 1))
+    low = 1
+    while low < by - 1:
+        ys = range(low, min(2 * low, by - 1))
+        low = ys[-1] + 1
         for y in ys:
             for j in range(2):
                 outer(j, y)
@@ -475,7 +476,8 @@
             pltpu.VMEM(permit.shape, f32), pltpu.VMEM(shift_diag.shape, f32),
             pltpu.VMEM(codes.shape, jnp.int32), pltpu.VMEM(counts.shape, jnp.int32), pltpu.VMEM(weights.shape, f32),
             pltpu.VMEM((order, order), f32),
-            pltpu.VMEM((bx, 9, by, coupling), f32), pltpu.VMEM((2, 3, by, coupling), f32),
+            pltpu.VMEM((bx, 9, by, coupling), f32),
+            pltpu.VMEM((2, 3, by, coupling), bf16), pltpu.VMEM((2, 3, by, coupling), bf16),
             pltpu.VMEM((2, by, packed, order), f32), pltpu.VMEM((2, by, packed, order), f32),
             pltpu.SemaphoreType.DMA((bx,)), pltpu.SemaphoreType.DMA((5,)),
             pltpu.SemaphoreType.DMA((copies,)), pltpu.SemaphoreType.DMA((copies,)),

time: 36.4 us -> 36 us (0.989)
  no operation moved by 1% of the time
where the time goes in v6:
time: 36 us; the launch traced here: 35.8 us
  Pallas kernels  34.4 us (96%)
  local copies, waits for them, and re-layouts  0.8 us (2%)
  between operations  0.66 us (2%)
    pallas_call x1, Pallas kernels, local(): pl.pallas_call(gram_kernel, out_shape=(pltpu.VMEM((bx, by, order, order),...  15.8 us
    pallas_call x1, Pallas kernels, local(): pl.pallas_call(sum_kernel, out_shape=pltpu.VMEM((bx, by, order, nv), bf16...  9.49 us
    pallas_call x1, Pallas kernels, local(): pl.pallas_call(factor_kernel, out_shape=(jax.ShapeDtypeStruct((bx, by, or...  9.05 us
    unnamed x1, local copies, waits for them, and re-layouts  0.8 us

profile of v6, /device:TPU:0, one launch (start us, length us, event | category | flops | bytes accessed | tf_op | source)
XLA Modules:
  0.0 35.8 jit_solution(17790655748066171148)
XLA Ops:
  0.6 15.8 %gram.1 = (f32[2,8,128,128]{3,2,1,0:T(8,128)S(1)}, f32[9,2,8,128]{3,2,1,0:T(8,128)S(1)}) custom-call(bf16[2,8,256,128]{3,2,1,0:T(8,128)(2,1)} %c_ref.1, f32[2,8,256]{2,1,0:T(8,128)} %permit_ref.1, f32[2,8,128]{2,1,0:T(8,128)} %shift_ref.1, s32[6,2,8]{2,1,0:T(2,128)} %bitcast.2, s32[2,8]{1,0:T(2,128)} %counts_ref.1, f32[6,2,8]{2,1,0:T(2,128)} %bitcast.3), custom_call_target="tpu_custom_call" | custom-call | tf_op jit(solution)/shard_map/gram/pallas_call | solution.py:468
  16.5 9.0 %factor.1 = (bf16[2,8,128,128]{3,2,1,0:T(8,128)(2,1)}, bf16[2,8,128,128]{3,2,1,0:T(8,128)(2,1)S(1)}, bf16[2,8,128,128]{3,2,1,0:T(8,128)(2,1)S(1)}) custom-call(f32[2,8,128,128]{3,2,1,0:T(8,128)S(1)} %get-tuple-element.7.gram_ref, bf16[2,8,128,128]{3,2,1,0:T(8,128)(2,1)} %v_ref.1), custom_call_target="tpu_custom_call" | custom-call | tf_op jit(solution)/shard_map/factor/pallas_call | solution.py:488
  25.5 9.5 %sums.1 = bf16[2,8,128,128]{3,2,1,0:T(8,128)(2,1)S(1)} custom-call(bf16[2,8,128,128]{3,2,1,0:T(8,128)(2,1)S(1)} %get-tuple-element.9.fac_ref, bf16[2,8,128,128]{3,2,1,0:T(8,128)(2,1)S(1)} %get-tuple-element.10.v_ref, f32[9,2,8,128]{3,2,1,0:T(8,128)S(1)} %get-tuple-element.11.wt), custom_call_target="tpu_custom_call" | custom-call | tf_op jit(solution)/shard_map/sums/pallas_call | solution.py:505
  35.0 0.8 %copy.10 = bf16[2,8,128,128]{3,2,1,0:T(8,128)(2,1)} copy(bf16[2,8,128,128]{3,2,1,0:T(8,128)(2,1)S(1)} %sums.1) | data formatting | bytes 1048576
